TPU v7x, 256 devices: a whole 4x4x8 slice. The times are simulated.
256 devices in a mesh: region: 128 (over z_hi, x, y, core), split: 2 (over z_lo).
Axes of the slice: x: 4, y: 4, z: 8 (z_hi: 4, z_lo: 2; z = z_hi * 2 + z_lo), core: 2. Of those that a mesh axis runs over, the one named last changes fastest.
Arguments:
- features: bfloat16 [96, 131072], P(None, ('region', 'split')), may hold values from -6 to 6
- kernel_one: bfloat16 [27, 96, 96], replicated, may hold values from -0.125 to 0.125
- kernel_two: bfloat16 [27, 96, 192], replicated, may hold values from -0.125 to 0.125
- occupancy: int32 [256, 512], P(('region', 'split')), may hold values 0 or 1
- neighbors: int32 [256, 27], P(('region', 'split')), may hold values from -1 to 255, as said below
- cotangent: bfloat16 [192, 131072], P(None, ('region', 'split')), may hold values from -0.016479492 to 0.016479492
Outputs:
- output: bfloat16 [192, 131072], P(None, ('region', 'split'))
- grad_one: float32 [27, 96, 96], replicated
- grad_two: float32 [27, 96, 192], replicated
Inputs may be any that keep to these rules, and one draw needn't show every extreme that they name: `neighbors`: entry k = 9 (dx + 1) + 3 (dy + 1) + (dz + 1) of a block's row is the active block whose block coordinates differ by (dx, dy, dz), or -1 if there is none; entry 13 is the block itself. Blocks are numbered in device order. The blocks of region r have x coordinate r and y coordinate 0 or 1; the device of split index s holds the blocks with z coordinate s. So a neighbour in region r - 1 or r + 1 differs by dx = -1 or +1, and a neighbour on the other device of the same region lies across the z boundary between the two halves.
All inputs are finite; a program needn't handle non-finite values. No bound on the sum of `occupancy` on one device may be relied on, other than what follows from the above.
Results may differ from a plain program's by a relative error of at most 0.0049.
Values may be sent and summed in bfloat16 or wider, within the bound.
A program may use at most 64 MiB of HBM per device.

v0:
```python
import jax
import jax.numpy as jnp
import numpy as np
from jax import lax
from jax.sharding import PartitionSpec as P


def padded(x, sides, width):
    for axis, dim in sides:
        count, length = (lax.axis_size(axis), x.shape[dim])
        up = [(i, (i + 1) % count) for i in range(count - 1)]
        down = [(j, i) for i, j in up]
        last = lax.slice_in_dim(x, length - width, length, axis=dim)
        first = lax.slice_in_dim(x, 0, width, axis=dim)
        before = lax.ppermute(last, axis, up)
        after = lax.ppermute(first, axis, down)
        x = jnp.concatenate([before, x, after], axis=dim)
    return x


def voxel_tables():
    voxels = np.arange(512)
    along_x = voxels // 64
    along_y = voxels // 8 % 8
    along_z = voxels % 8
    block_code = np.zeros((27, 512), np.int32)
    voxel_code = np.zeros((27, 512), np.int32)
    for offset in range(27):
        moved_x = along_x + offset // 9 - 1
        moved_y = along_y + offset // 3 % 3 - 1
        moved_z = along_z + offset % 3 - 1
        block_code[offset] = (moved_x // 8 + 1) * 9 + (moved_y // 8 + 1) * 3 + (moved_z // 8 + 1)
        voxel_code[offset] = moved_x % 8 * 64 + moved_y % 8 * 8 + moved_z % 8
    on_shell = (
        (along_x == 0)
        | (along_x == 7)
        | (along_y == 0)
        | (along_y == 7)
        | (along_z == 0)
        | (along_z == 7)
    )
    shell_voxels = voxels[on_shell].astype(np.int32)
    shell_slot = np.zeros(512, np.int32)
    shell_slot[shell_voxels] = np.arange(shell_voxels.shape[0], dtype=np.int32)
    return (block_code, voxel_code, shell_voxels, shell_slot)


def convolve(window_rows, lookup, kernel):

    def accumulate(offset, total):
        picked = jnp.take(
            window_rows, lax.dynamic_index_in_dim(lookup, offset, 0, keepdims=False), axis=0
        )
        weights = lax.dynamic_index_in_dim(kernel, offset, 0, keepdims=False)
        return total + jnp.dot(picked, weights, preferred_element_type=jnp.float32)

    return lax.fori_loop(
        0, 27, accumulate, jnp.zeros((lookup.shape[1], kernel.shape[2]), jnp.float32)
    )


def kernel_gradient(window_rows, lookup, gradient_rows):

    def accumulate(offset, total):
        picked = jnp.take(
            window_rows, lax.dynamic_index_in_dim(lookup, offset, 0, keepdims=False), axis=0
        )
        product = jnp.dot(picked.T, gradient_rows, preferred_element_type=jnp.float32)
        return lax.dynamic_update_index_in_dim(total, product, offset, 0)

    return lax.fori_loop(
        0,
        27,
        accumulate,
        jnp.zeros((27, window_rows.shape[1], gradient_rows.shape[1]), jnp.float32),
    )


def convolve_back(window_rows, lookup, kernel):

    def accumulate(offset, total):
        picked = jnp.take(
            window_rows, lax.dynamic_index_in_dim(lookup, 26 - offset, 0, keepdims=False), axis=0
        )
        weights = lax.dynamic_index_in_dim(kernel, offset, 0, keepdims=False)
        return total + jnp.dot(picked, weights.T, preferred_element_type=jnp.float32)

    return lax.fori_loop(
        0, 27, accumulate, jnp.zeros((lookup.shape[1], kernel.shape[1]), jnp.float32)
    )


def shards(features, kernel_one, kernel_two, occupancy, neighbors, cotangent):
    block_count = neighbors.shape[0]
    split_size = lax.axis_size("split")
    region_pos = lax.axis_index("region")
    window_first = (region_pos - 1) * split_size * block_count
    block_code, voxel_code, shell_voxels, shell_slot = voxel_tables()
    block_ids = jnp.transpose(jnp.take(neighbors, jnp.asarray(block_code), axis=1), (1, 0, 2))
    voxel_target = jnp.asarray(voxel_code)[:, None, :]
    window_cols = 3 * split_size * block_count * 512
    lookup = jnp.where(block_ids < 0, window_cols, (block_ids - window_first) * 512 + voxel_target)

    def spread(values):
        channels = values.shape[0]
        gathered = lax.all_gather(values, "split", axis=1, tiled=True)
        window = padded(gathered, (("region", 1),), gathered.shape[1])
        return jnp.concatenate([window, jnp.zeros((channels, 1), values.dtype)], axis=1).T

    lookup = lookup.reshape(27, -1).astype(jnp.int32)
    active = (occupancy.reshape(-1) > 0)[None, :]
    zero_value = jnp.zeros((), features.dtype)
    masked = jnp.where(active, features, zero_value)
    masked_window = spread(masked)
    hidden_pre = jnp.where(active, convolve(masked_window, lookup, kernel_one).T, 0.0)
    hidden = jnp.where(active, jax.nn.silu(hidden_pre), 0.0).astype(jnp.bfloat16)
    hidden_window = spread(hidden)
    output = jnp.where(active, convolve(hidden_window, lookup, kernel_two).T, 0.0)
    grad_out = jnp.where(active, cotangent, zero_value)
    grad_two = kernel_gradient(hidden_window, lookup, grad_out.T)
    back = convolve_back(spread(grad_out), lookup, kernel_two).T
    sigmoid_pre = jax.nn.sigmoid(hidden_pre)
    grad_pre = jnp.where(
        active, back * sigmoid_pre * (1.0 + hidden_pre * (1.0 - sigmoid_pre)), 0.0
    ).astype(jnp.bfloat16)
    grad_one = kernel_gradient(masked_window, lookup, grad_pre.T)
    grad_one, grad_two = lax.psum((grad_one, grad_two), ("region", "split"))
    return (output.astype(jnp.bfloat16), grad_one, grad_two)


def solution(mesh):
    in_specs = (
        P(None, ("region", "split")),
        P(),
        P(),
        P(("region", "split"), None),
        P(("region", "split"), None),
        P(None, ("region", "split")),
    )
    out_specs = (P(None, ("region", "split")), P(), P())
    return jax.shard_map(shards, mesh=mesh, in_specs=in_specs, out_specs=out_specs, check_vma=False)
```

profile of v0, /device:TPU:2, one launch (start us, length us, event | category | flops | bytes accessed | tf_op | source)
XLA Modules:
  0.0 733.8 jit_solution(8820615939577342043)
XLA Ops:
  8.8 5.4 all_gather.9
  14.2 3.6 collective-permute-start.1
  21.0 8.9 %all_gather.11 = bf16[192,1024]{0,1:T(8,128)(2,1)S(1)} all-gather(bf16[192,512]{0,1:T(8,128)(2,1)S(1)} %broadcast_select_fusion), channel_id=1, replica_groups=mesh['region'=128,'split'=2] {'split'}, dimensions={1}, use_global_device_ids=true | all-gather | bytes 589824 | tf_op jit(solution)/shard_map/all_gather | solution.py:106
  29.9 4.0 collective-permute-start.5
  35.9 77.0 %gather_fusion.5 = s32[13824]{0:T(1024)S(1)} fusion(s32[27]{0:T(128)S(1)} %bitcast.83, s32[14336]{0:T(1024)S(1)} %pad_clamp_fusion.5), kind=kCustom, calls=%fused_computation.5 | custom fusion | bytes 165888 | tf_op jit(solution)/shard_map/jit(_take)/gather | solution.py:99
  113.6 67.2 %while.72 = (s32[]{:T(128)}, f32[512,96]{0,1:T(8,128)S(1)}, s32[27,512]{1,0:T(8,128)S(1)}, bf16[3073,96]{1,0:T(8,128)(2,1)S(1)}, bf16[27,96,96]{2,1,0:T(8,128)(2,1)}, /*index=5*/s32[]{:T(128)}, s32[]{:T(128)}) while((s32[]{:T(128)}, f32[512,96]{0,1:T(8,128)S(1)}, s32[27,512]{1,0:T(8,128)S(1)}, bf16[3073,96]{1,0:T(8,128)(2,1)S(1)}, ...), condition=%wide.region_1.3_spmd.clone, body=%wide.region_0.0_spmd.clone.sunk | while | flops 9590275 | bytes 732263 | solution.py:57
  180.8 5.3 all_gather.10
  186.1 4.7 collective-permute-start.3
  194.0 5.9 collective-permute-done.2
  203.1 106.1 %while.74 = (s32[]{:T(128)}, f32[512,96]{0,1:T(8,128)}, s32[27,512]{1,0:T(8,128)S(1)}, bf16[3073,192]{1,0:T(8,128)(2,1)S(1)}, bf16[27,96,192]{2,1,0:T(8,128)(2,1...) while((s32[]{:T(128)}, f32[512,96]{0,1:T(8,128)}, s32[27,512]{1,0:T(8,128)S(1)}, ...), condition=%wide.region_5.7_spmd.clone, body=%wide.region_4.6_spmd.clone.sunk | while | flops 19076616 | bytes 1049765 | solution.py:88
  203.2 2.0 gather_fusion.4
  206.9 2.0 gather_fusion.4
  208.9 1.9 convolution_add_fusion.8
  210.9 2.0 gather_fusion.4
  212.8 1.9 convolution_add_fusion.8
  214.8 2.0 gather_fusion.4
  216.8 1.9 convolution_add_fusion.8
  218.7 2.0 gather_fusion.4
  220.7 1.9 convolution_add_fusion.8
  222.7 2.0 gather_fusion.4
  224.6 1.9 convolution_add_fusion.8
  226.6 2.0 gather_fusion.4
  228.6 1.9 convolution_add_fusion.8
  230.5 2.0 gather_fusion.4
  232.5 1.9 convolution_add_fusion.8
  234.5 2.0 gather_fusion.4
  236.4 1.9 convolution_add_fusion.8
  238.4 2.0 gather_fusion.4
  240.4 1.9 convolution_add_fusion.8
  242.3 2.0 gather_fusion.4
  244.3 1.9 convolution_add_fusion.8
  246.3 2.0 gather_fusion.4
  248.2 1.9 convolution_add_fusion.8
  250.2 2.0 gather_fusion.4
  252.2 1.9 convolution_add_fusion.8
  254.2 2.0 gather_fusion.4
  256.1 1.9 convolution_add_fusion.8
  258.1 2.0 gather_fusion.4
  260.0 1.9 convolution_add_fusion.8
  262.0 2.0 gather_fusion.4
  264.0 1.9 convolution_add_fusion.8
  266.0 2.0 gather_fusion.4
  267.9 1.9 convolution_add_fusion.8
  269.9 2.0 gather_fusion.4
  271.9 1.9 convolution_add_fusion.8
  273.8 2.0 gather_fusion.4
  277.8 2.0 gather_fusion.4
  279.7 1.9 convolution_add_fusion.8
  281.7 2.0 gather_fusion.4
  283.7 1.9 convolution_add_fusion.8
  285.6 2.0 gather_fusion.4
  287.6 1.9 convolution_add_fusion.8
  289.6 2.0 gather_fusion.4
  293.5 2.0 gather_fusion.4
  295.5 1.9 convolution_add_fusion.8
  297.4 2.0 gather_fusion.4
  299.4 1.9 convolution_add_fusion.8
  301.4 2.0 gather_fusion.4
  305.3 2.0 gather_fusion.4
  310.5 63.1 %while.70 = (s32[]{:T(128)}, f32[27,96,96]{2,1,0:T(8,128)}, s32[27,512]{1,0:T(8,128)S(1)}, bf16[3073,96]{1,0:T(8,128)(2,1)S(1)}, bf16[512,96]{1,0:T(8,128)(2,1)S(1)}, /*index=5*/s32[]{:T(128)}) while((s32[]{:T(128)}, f32[27,96,96]{2,1,0:T(8,128)}, s32[27,512]{1,0:T(8,128)S(1)}, bf16[3073,96]{1,0:T(8,128)(2,1)S(1)}, ...), condition=%wide.region_7.9_spmd, body=%wide.region_6.8_spmd.sunk | while | flops 9491970 | bytes 461909 | solution.py:71
  373.6 63.7 %while.71 = (s32[]{:T(128)}, f32[27,96,192]{2,1,0:T(8,128)}, s32[27,512]{1,0:T(8,128)S(1)}, bf16[3073,96]{1,0:T(8,128)(2,1)S(1)}, bf16[512,192]{1,0:T(8,128)(2,1)S(1)}, /*index=5*/s32[]{:T(128)}) while((s32[]{:T(128)}, f32[27,96,192]{2,1,0:T(8,128)}, s32[27,512]{1,0:T(8,128)S(1)}, bf16[3073,96]{1,0:T(8,128)(2,1)S(1)}, ...), condition=%wide.region_10.12_spmd, body=%wide.region_9.11_spmd.sunk | while | flops 18929152 | bytes 609365 | solution.py:71
  438.3 69.8 %while.73 = (s32[]{:T(128)}, f32[512,192]{0,1:T(8,128)S(1)}, s32[27,512]{1,0:T(8,128)S(1)}, bf16[3073,96]{1,0:T(8,128)(2,1)S(1)}, bf16[27,96,192]{2,1,0:T(8,128)(2,1)}, /*index=5*/s32[]{:T(128)}, s32[]{:T(128)}) while((s32[]{:T(128)}, f32[512,192]{0,1:T(8,128)S(1)}, s32[27,512]{1,0:T(8,128)S(1)}, bf16[3073,96]{1,0:T(8,128)(2,1)S(1)}, ...), condition=%wide.region_3.5_spmd.clone, body=%wide.region_2.4_spmd.clone.sunk | while | flops 19125764 | bytes 1150055 | solution.py:57
  508.8 214.0 %all-reduce.3.cloned.1.call-done = (f32[27,96,96]{2,1,0:T(8,128)}, f32[27,96,192]{2,1,0:T(8,128)}) async-done(((f32[27,96,96]{2,1,0:T(8,128)}, f32[27,96,192]{2,1,0:T(8,128)}), (f32[27,96,96]{2,1,0:T(8,128)}, f32[27,96,192]{2,1,0:T(8,128)})) %all-reduce.3.cloned.1.call-update) | async-done | bytes 2986000 | tf_op jit(solution)/shard_map/psum | solution.py:127
  722.9 2.6 copy.57
  (786 shorter events, 287.3 us)
Async XLA Ops:
  7.2 28.7 %copy-start = (s32[1,27]{1,0:T(1,128)S(1)}, s32[1,27]{1,0:T(1,128)}, u32[]{:S(2)}) copy-start(s32[1,27]{1,0:T(1,128)} %param.24) | copy-start | bytes 328
  7.2 28.7 %copy-start.7 = (s32[13824]{0:T(1024)S(1)}, s32[13824]{0:T(1024)}, u32[]{:S(2)}) copy-start(s32[13824]{0:T(1024)} %constant.268) | copy-start | bytes 165892
  7.2 715.7 %all-reduce.3.cloned.1.call-start = ((), (), s32[]{:S(2)}) async-start(), calls=%async_computation | async-start | bytes 7962624 | tf_op jit(solution)/shard_map/psum | solution.py:127
  14.2 98.8 %collective-permute-start.1 = (bf16[96,1024]{1,0:T(8,128)(2,1)S(1)}, bf16[96,1024]{1,0:T(8,128)(2,1)S(1)}, u32[]{:S(2)}, u32[]{:S(2)}) collective-permute-start(bf16[96,1024]{1,0:T(8,128)(2,1)S(1)} %all_gather.9), channel_id=1, source_target_pairs={{2,0},{4,2},{6,4},{8,6},{10,8},{12,10},{14,12},{16,14},{18,16},{20... | collective-permute-start | bytes 589832 | tf_op jit(solution)/shard_map/ppermute | solution.py:16
  17.9 95.2 %collective-permute-start = (bf16[96,1024]{1,0:T(8,128)(2,1)S(1)}, bf16[96,1024]{1,0:T(8,128)(2,1)S(1)}, u32[]{:S(2)}, u32[]{:S(2)}) collective-permute-start(bf16[96,1024]{1,0:T(8,128)(2,1)S(1)} %all_gather.9), channel_id=1, source_target_pairs={{0,2},{2,4},{4,6},{6,8},{8,10},{10,12},{12,14},{14,16},{16,18},{18... | collective-permute-start | bytes 589832 | tf_op jit(solution)/shard_map/ppermute | solution.py:15
  29.9 83.0 %copy-start.5 = (bf16[192,1024]{0,1:T(8,128)(2,1)}, bf16[192,1024]{0,1:T(8,128)(2,1)S(1)}, u32[]{:S(2)}) copy-start(bf16[192,1024]{0,1:T(8,128)(2,1)S(1)} %all_gather.11) | copy-start | bytes 1179652
  29.9 170.5 %collective-permute-start.5 = (bf16[192,1024]{0,1:T(8,128)(2,1)S(1)}, bf16[192,1024]{0,1:T(8,128)(2,1)S(1)}, u32[]{:S(2)}, u32[]{:S(2)}) collective-permute-start(bf16[192,1024]{0,1:T(8,128)(2,1)S(1)} %all_gather.11), channel_id=1, source_target_pairs={{2,0},{4,2},{6,4},{8,6},{10,8},{12,10},{14,12},{16,14},{18,16},{20... | collective-permute-start | bytes 1179656 | tf_op jit(solution)/shard_map/ppermute | solution.py:16
  33.9 167.3 %collective-permute-start.4 = (bf16[192,1024]{0,1:T(8,128)(2,1)S(1)}, bf16[192,1024]{0,1:T(8,128)(2,1)}, u32[]{:S(2)}, u32[]{:S(2)}) collective-permute-start(bf16[192,1024]{0,1:T(8,128)(2,1)S(1)} %all_gather.11), channel_id=1, source_target_pairs={{0,2},{2,4},{4,6},{6,8},{8,10},{10,12},{12,14},{14,16},{16,18},{18... | collective-permute-start | bytes 1179656 | tf_op jit(solution)/shard_map/ppermute | solution.py:15
  35.9 77.0 %copy-start.8 = (s32[13824]{0:T(1024)S(1)}, s32[13824]{0:T(1024)}, u32[]{:S(2)}) copy-start(s32[13824]{0:T(1024)} %constant.270) | copy-start | bytes 165892
  180.8 19.1 %copy-start.2 = (f32[512,96]{0,1:T(8,128)}, f32[512,96]{0,1:T(8,128)S(1)}, u32[]{:S(2)}) copy-start(f32[512,96]{0,1:T(8,128)S(1)} %get-tuple-element.512) | copy-start | bytes 589828
  186.1 7.8 %collective-permute-start.3 = (bf16[96,1024]{1,0:T(8,128)(2,1)S(1)}, bf16[96,1024]{1,0:T(8,128)(2,1)S(1)}, u32[]{:S(2)}, u32[]{:S(2)}) collective-permute-start(bf16[96,1024]{1,0:T(8,128)(2,1)S(1)} %all_gather.10), channel_id=1, source_target_pairs={{2,0},{4,2},{6,4},{8,6},{10,8},{12,10},{14,12},{16,14},{18,16},{20... | collective-permute-start | bytes 589832 | tf_op jit(solution)/shard_map/ppermute | solution.py:16
  190.8 9.1 %collective-permute-start.2 = (bf16[96,1024]{1,0:T(8,128)(2,1)S(1)}, bf16[96,1024]{1,0:T(8,128)(2,1)S(1)}, u32[]{:S(2)}, u32[]{:S(2)}) collective-permute-start(bf16[96,1024]{1,0:T(8,128)(2,1)S(1)} %all_gather.10), channel_id=1, source_target_pairs={{0,2},{2,4},{4,6},{6,8},{8,10},{10,12},{12,14},{14,16},{16,18},{18... | collective-permute-start | bytes 589832 | tf_op jit(solution)/shard_map/ppermute | solution.py:15
  200.4 0.8 copy-start.6
  310.4 63.2 %copy-start.3 = (bf16[512,192]{1,0:T(8,128)(2,1)S(1)}, bf16[512,192]{1,0:T(8,128)(2,1)}, u32[]{:S(2)}) copy-start(bf16[512,192]{1,0:T(8,128)(2,1)} %fusion.39) | copy-start | bytes 589828
  437.3 1.0 copy-start.1
  722.9 2.6 copy-start.4
Sparse Core Ops, SparseCore 0:
  437.4 285.4 all-reduce.2
where the time goes:
time: 738 us; the launch traced here: 734 us
  local copies, waits for them, and re-layouts  283 us (38%)
  waiting for transfers between devices  220 us (30%)
  matrix products  164 us (22%)
  blocking collectives  19.6 us (3%)
  starting transfers between devices  18.1 us (2%)
  between operations  14.4 us (2%)
  other arithmetic  9.17 us (1%)
    psum x1, waiting for transfers between devices, shards(): grad_one, grad_two = lax.psum((grad_one, grad_two), ('region', 'split'))  214 us
    gather x108, local copies, waits for them, and re-layouts, accumulate(): jnp.take(window_rows, lax.dynamic_index_in_dim(lookup, offset, 0, keepdim...  145 us
    gather x1, local copies, waits for them, and re-layouts, shards(): jnp.take(neighbors, jnp.asarray(block_code), axis=1)  77 us
    dot_general x54, matrix products, accumulate(): return total + jnp.dot(picked, weights, preferred_element_type=jnp.float32)  59.8 us
    gather x27, local copies, waits for them, and re-layouts, accumulate(): jnp.take(window_rows, lax.dynamic_index_in_dim(lookup, 26 - offset, 0, ke...  52.7 us
    dot_general x27, matrix products, accumulate(): jnp.dot(picked, weights.T, preferred_element_type=jnp.float32)  52.1 us
    dot_general x54, matrix products, accumulate(): jnp.dot(picked.T, gradient_rows, preferred_element_type=jnp.float32)  51.7 us
    all_gather x3, blocking collectives, spread(): gathered = lax.all_gather(values, 'split', axis=1, tiled=True)  19.6 us
  transfers between devices with their start and end apart: 7, of which 3 were waited for; matrix products, arithmetic and copies ran while one was open for 29% of the time, Pallas kernels for 0%

commit v1 on v0

--- a/solution.py
+++ b/solution.py
@@ -124,7 +124,7 @@
         active, back * sigmoid_pre * (1.0 + hidden_pre * (1.0 - sigmoid_pre)), 0.0
     ).astype(jnp.bfloat16)
     grad_one = kernel_gradient(masked_window, lookup, grad_pre.T)
-    grad_one, grad_two = lax.psum((grad_one, grad_two), ("region", "split"))
+    grad_one, grad_two = lax.psum(lax.psum((grad_one, grad_two), "split"), "region")
     return (output.astype(jnp.bfloat16), grad_one, grad_two)
 
 

time: 738 us -> 1940 us (2.63); the launches traced: 734 us -> 1910 us
  waiting for transfers between devices: 220 us -> 1400 us
    psum x1 -> x2, waiting for transfers between devices: 214 us -> 1390 us  [the longest x1 1270 us: shards(): lax.psum(lax.psum((grad_one, grad_two), 'split'), 'region')]
  transfers between devices with their start and end apart: 7 -> 8, of which waited for: 3 -> 4; matrix products, arithmetic and copies ran while one was open for 29% -> 11% of each run, Pallas kernels for 0% -> 0%
where the time goes in v1:
time: 1940 us; the launch traced here: 1910 us
  waiting for transfers between devices  1400 us (72%)
  local copies, waits for them, and re-layouts  282 us (15%)
  matrix products  164 us (8%)
  blocking collectives  19.6 us (1%)
    psum x1, waiting for transfers between devices, shards(): lax.psum(lax.psum((grad_one, grad_two), 'split'), 'region')  1270 us
    gather x108, local copies, waits for them, and re-layouts, accumulate(): jnp.take(window_rows, lax.dynamic_index_in_dim(lookup, offset, 0, keepdim...  145 us
    psum x1, waiting for transfers between devices, shards(): lax.psum((grad_one, grad_two), 'split')  129 us
    gather x1, local copies, waits for them, and re-layouts, shards(): jnp.take(neighbors, jnp.asarray(block_code), axis=1)  77 us
    dot_general x54, matrix products, accumulate(): return total + jnp.dot(picked, weights, preferred_element_type=jnp.float32)  59.8 us
    gather x27, local copies, waits for them, and re-layouts, accumulate(): jnp.take(window_rows, lax.dynamic_index_in_dim(lookup, 26 - offset, 0, ke...  52.7 us
    dot_general x27, matrix products, accumulate(): jnp.dot(picked, weights.T, preferred_element_type=jnp.float32)  52.1 us
    dot_general x54, matrix products, accumulate(): jnp.dot(picked.T, gradient_rows, preferred_element_type=jnp.float32)  51.7 us
  transfers between devices with their start and end apart: 8, of which 4 were waited for; matrix products, arithmetic and copies ran while one was open for 11% of the time, Pallas kernels for 0%

profile of v1, /device:TPU:2, one launch (start us, length us, event | category | flops | bytes accessed | tf_op | source)
XLA Modules:
  0.0 1913.6 jit_solution(3622494542035522460)
XLA Ops:
  8.8 5.4 all_gather.9
  14.2 3.6 collective-permute-start.1
  21.0 8.9 all_gather.11
  29.9 4.0 collective-permute-start.5
  35.9 77.0 %gather_fusion.5 = s32[13824]{0:T(1024)S(1)} fusion(s32[27]{0:T(128)S(1)} %bitcast.83, s32[14336]{0:T(1024)S(1)} %pad_clamp_fusion.5), kind=kCustom, calls=%fused_computation.5 | custom fusion | bytes 165888 | tf_op jit(solution)/shard_map/jit(_take)/gather | solution.py:99
  113.6 67.1 %while.72 = (s32[]{:T(128)}, f32[512,96]{0,1:T(8,128)S(1)}, s32[27,512]{1,0:T(8,128)S(1)}, bf16[3073,96]{1,0:T(8,128)(2,1)S(1)}, bf16[27,96,96]{2,1,0:T(8,128)(2,1)}, /*index=5*/s32[]{:T(128)}, s32[]{:T(128)}) while((s32[]{:T(128)}, f32[512,96]{0,1:T(8,128)S(1)}, s32[27,512]{1,0:T(8,128)S(1)}, bf16[3073,96]{1,0:T(8,128)(2,1)S(1)}, ...), condition=%wide.region_1.3_spmd.clone, body=%wide.region_0.0_spmd.clone.sunk | while | flops 9590275 | bytes 732263 | solution.py:57
  180.8 5.3 all_gather.10
  186.0 4.7 collective-permute-start.3
  193.9 5.9 collective-permute-done.2
  203.0 106.1 %while.74 = (s32[]{:T(128)}, f32[512,96]{0,1:T(8,128)}, s32[27,512]{1,0:T(8,128)S(1)}, bf16[3073,192]{1,0:T(8,128)(2,1)S(1)}, bf16[27,96,192]{2,1,0:T(8,128)(2,1...) while((s32[]{:T(128)}, f32[512,96]{0,1:T(8,128)}, s32[27,512]{1,0:T(8,128)S(1)}, ...), condition=%wide.region_5.7_spmd.clone, body=%wide.region_4.6_spmd.clone.sunk | while | flops 19076616 | bytes 1049765 | solution.py:88
  203.1 2.0 gather_fusion.4
  206.9 2.0 gather_fusion.4
  208.9 1.9 convolution_add_fusion.8
  210.8 2.0 gather_fusion.4
  212.8 1.9 convolution_add_fusion.8
  214.8 2.0 gather_fusion.4
  216.7 1.9 convolution_add_fusion.8
  218.7 2.0 gather_fusion.4
  220.7 1.9 convolution_add_fusion.8
  222.6 2.0 gather_fusion.4
  224.6 1.9 convolution_add_fusion.8
  226.6 2.0 gather_fusion.4
  228.5 1.9 convolution_add_fusion.8
  230.5 2.0 gather_fusion.4
  232.5 1.9 convolution_add_fusion.8
  234.4 2.0 gather_fusion.4
  236.4 1.9 convolution_add_fusion.8
  238.4 2.0 gather_fusion.4
  240.3 1.9 convolution_add_fusion.8
  242.3 2.0 gather_fusion.4
  244.3 1.9 convolution_add_fusion.8
  246.2 2.0 gather_fusion.4
  248.2 1.9 convolution_add_fusion.8
  250.2 2.0 gather_fusion.4
  252.1 1.9 convolution_add_fusion.8
  254.1 2.0 gather_fusion.4
  256.1 1.9 convolution_add_fusion.8
  258.1 2.0 gather_fusion.4
  260.0 1.9 convolution_add_fusion.8
  262.0 2.0 gather_fusion.4
  263.9 1.9 convolution_add_fusion.8
  265.9 2.0 gather_fusion.4
  269.9 2.0 gather_fusion.4
  271.8 1.9 convolution_add_fusion.8
  273.8 2.0 gather_fusion.4
  275.8 1.9 convolution_add_fusion.8
  277.7 2.0 gather_fusion.4
  281.7 2.0 gather_fusion.4
  285.6 2.0 gather_fusion.4
  287.6 1.9 convolution_add_fusion.8
  289.5 2.0 gather_fusion.4
  291.5 1.9 convolution_add_fusion.8
  293.5 2.0 gather_fusion.4
  297.4 2.0 gather_fusion.4
  299.4 1.9 convolution_add_fusion.8
  301.3 2.0 gather_fusion.4
  303.3 1.9 convolution_add_fusion.8
  305.3 2.0 gather_fusion.4
  310.4 63.1 %while.70 = (s32[]{:T(128)}, f32[27,96,96]{2,1,0:T(8,128)}, s32[27,512]{1,0:T(8,128)S(1)}, bf16[3073,96]{1,0:T(8,128)(2,1)S(1)}, bf16[512,96]{1,0:T(8,128)(2,1)S(1)}, /*index=5*/s32[]{:T(128)}) while((s32[]{:T(128)}, f32[27,96,96]{2,1,0:T(8,128)}, s32[27,512]{1,0:T(8,128)S(1)}, bf16[3073,96]{1,0:T(8,128)(2,1)S(1)}, ...), condition=%wide.region_7.9_spmd, body=%wide.region_6.8_spmd.sunk | while | flops 9491970 | bytes 461909 | solution.py:71
  373.5 63.6 %while.71 = (s32[]{:T(128)}, f32[27,96,192]{2,1,0:T(8,128)}, s32[27,512]{1,0:T(8,128)S(1)}, bf16[3073,96]{1,0:T(8,128)(2,1)S(1)}, bf16[512,192]{1,0:T(8,128)(2,1)S(1)}, /*index=5*/s32[]{:T(128)}) while((s32[]{:T(128)}, f32[27,96,192]{2,1,0:T(8,128)}, s32[27,512]{1,0:T(8,128)S(1)}, bf16[3073,96]{1,0:T(8,128)(2,1)S(1)}, ...), condition=%wide.region_11.13_spmd, body=%wide.region_10.12_spmd.sunk | while | flops 18929152 | bytes 609365 | solution.py:71
  437.2 128.9 %all-reduce.7.cloned.1.call-done = (f32[27,96,96]{2,1,0:T(8,128)}, f32[27,96,192]{2,1,0:T(8,128)}) async-done(((f32[27,96,96]{2,1,0:T(8,128)}, f32[27,96,192]{2,1,0:T(8,128)}), (f32[27,96,96]{2,1,0:T(8,128)}, f32[27,96,192]{2,1,0:T(8,128)})) %all-reduce.7.cloned.1.call-update) | async-done | bytes 2986000 | tf_op jit(solution)/shard_map/psum | solution.py:127
  566.2 69.9 %while.73 = (s32[]{:T(128)}, f32[512,192]{0,1:T(8,128)S(1)}, s32[27,512]{1,0:T(8,128)S(1)}, bf16[3073,96]{1,0:T(8,128)(2,1)S(1)}, bf16[27,96,192]{2,1,0:T(8,128)(2,1)}, /*index=5*/s32[]{:T(128)}, s32[]{:T(128)}) while((s32[]{:T(128)}, f32[512,192]{0,1:T(8,128)S(1)}, s32[27,512]{1,0:T(8,128)S(1)}, bf16[3073,96]{1,0:T(8,128)(2,1)S(1)}, ...), condition=%wide.region_3.5_spmd.clone, body=%wide.region_2.4_spmd.clone.sunk | while | flops 19125764 | bytes 1150055 | solution.py:57
  636.8 1265.8 %all-reduce.5.cloned.1.call-done = (f32[27,96,96]{2,1,0:T(8,128)}, f32[27,96,192]{2,1,0:T(8,128)}) async-done(((f32[27,96,96]{2,1,0:T(8,128)}, f32[27,96,192]{2,1,0:T(8,128)}), (f32[27,96,96]{2,1,0:T(8,128)}, f32[27,96,192]{2,1,0:T(8,128)})) %all-reduce.5.cloned.1.call-update) | async-done | bytes 2986000 | tf_op jit(solution)/shard_map/psum | solution.py:127
  1902.6 2.6 copy.59
  (787 shorter events, 288.3 us)
Async XLA Ops:
  7.2 28.7 %copy-start = (s32[1,27]{1,0:T(1,128)S(1)}, s32[1,27]{1,0:T(1,128)}, u32[]{:S(2)}) copy-start(s32[1,27]{1,0:T(1,128)} %param.24) | copy-start | bytes 328
  7.2 28.7 %copy-start.6 = (s32[13824]{0:T(1024)S(1)}, s32[13824]{0:T(1024)}, u32[]{:S(2)}) copy-start(s32[13824]{0:T(1024)} %constant.268) | copy-start | bytes 165892
  7.2 559.0 %all-reduce.7.cloned.1.call-start = ((), (), s32[]{:S(2)}) async-start(), calls=%async_computation.1 | async-start | bytes 7962624 | tf_op jit(solution)/shard_map/psum | solution.py:127
  14.2 98.8 %collective-permute-start.1 = (bf16[96,1024]{1,0:T(8,128)(2,1)S(1)}, bf16[96,1024]{1,0:T(8,128)(2,1)S(1)}, u32[]{:S(2)}, u32[]{:S(2)}) collective-permute-start(bf16[96,1024]{1,0:T(8,128)(2,1)S(1)} %all_gather.9), channel_id=1, source_target_pairs={{2,0},{4,2},{6,4},{8,6},{10,8},{12,10},{14,12},{16,14},{18,16},{20... | collective-permute-start | bytes 589832 | tf_op jit(solution)/shard_map/ppermute | solution.py:16
  17.9 95.2 %collective-permute-start = (bf16[96,1024]{1,0:T(8,128)(2,1)S(1)}, bf16[96,1024]{1,0:T(8,128)(2,1)S(1)}, u32[]{:S(2)}, u32[]{:S(2)}) collective-permute-start(bf16[96,1024]{1,0:T(8,128)(2,1)S(1)} %all_gather.9), channel_id=1, source_target_pairs={{0,2},{2,4},{4,6},{6,8},{8,10},{10,12},{12,14},{14,16},{16,18},{18... | collective-permute-start | bytes 589832 | tf_op jit(solution)/shard_map/ppermute | solution.py:15
  29.9 83.0 %copy-start.4 = (bf16[192,1024]{0,1:T(8,128)(2,1)}, bf16[192,1024]{0,1:T(8,128)(2,1)S(1)}, u32[]{:S(2)}) copy-start(bf16[192,1024]{0,1:T(8,128)(2,1)S(1)} %all_gather.11) | copy-start | bytes 1179652
  29.9 170.5 %collective-permute-start.5 = (bf16[192,1024]{0,1:T(8,128)(2,1)S(1)}, bf16[192,1024]{0,1:T(8,128)(2,1)S(1)}, u32[]{:S(2)}, u32[]{:S(2)}) collective-permute-start(bf16[192,1024]{0,1:T(8,128)(2,1)S(1)} %all_gather.11), channel_id=1, source_target_pairs={{2,0},{4,2},{6,4},{8,6},{10,8},{12,10},{14,12},{16,14},{18,16},{20... | collective-permute-start | bytes 1179656 | tf_op jit(solution)/shard_map/ppermute | solution.py:16
  33.9 167.3 %collective-permute-start.4 = (bf16[192,1024]{0,1:T(8,128)(2,1)S(1)}, bf16[192,1024]{0,1:T(8,128)(2,1)}, u32[]{:S(2)}, u32[]{:S(2)}) collective-permute-start(bf16[192,1024]{0,1:T(8,128)(2,1)S(1)} %all_gather.11), channel_id=1, source_target_pairs={{0,2},{2,4},{4,6},{6,8},{8,10},{10,12},{12,14},{14,16},{16,18},{18... | collective-permute-start | bytes 1179656 | tf_op jit(solution)/shard_map/ppermute | solution.py:15
  35.9 77.0 %copy-start.7 = (s32[13824]{0:T(1024)S(1)}, s32[13824]{0:T(1024)}, u32[]{:S(2)}) copy-start(s32[13824]{0:T(1024)} %constant.270) | copy-start | bytes 165892
  180.7 19.2 %copy-start.1 = (f32[512,96]{0,1:T(8,128)}, f32[512,96]{0,1:T(8,128)S(1)}, u32[]{:S(2)}) copy-start(f32[512,96]{0,1:T(8,128)S(1)} %get-tuple-element.512) | copy-start | bytes 589828
  186.0 7.8 collective-permute-start.3
  190.7 9.1 collective-permute-start.2
  200.4 0.8 copy-start.5
  310.4 63.1 %copy-start.2 = (bf16[512,192]{1,0:T(8,128)(2,1)S(1)}, bf16[512,192]{1,0:T(8,128)(2,1)}, u32[]{:S(2)}) copy-start(bf16[512,192]{1,0:T(8,128)(2,1)} %fusion.39) | copy-start | bytes 589828
  437.2 1465.4 %all-reduce.5.cloned.1.call-start = ((), (), s32[]{:S(2)}) async-start(), calls=%async_computation | async-start | bytes 7962624 | tf_op jit(solution)/shard_map/psum | solution.py:127
  1902.6 2.6 copy-start.3
Sparse Core Ops, SparseCore 0:
  437.3 128.8 all-reduce.6
  568.9 1333.6 all-reduce.4
